TPU v7x, 512 devices: a whole 4x8x8 slice. The times are simulated.
512 devices in a mesh: item: 16 (over y, core), user: 32 (over z, x).
Axes of the slice: x: 4, y: 8, z: 8, core: 2. Of those that a mesh axis runs over, the one named last changes fastest.
Arguments:
- item_factors: float32 [32768, 128], P('item')
- tile_lists: int32 [512, 16], P(('item', 'user')), may hold values from 0 to 255, as said below
- tile_weights: bfloat16 [512, 16, 128, 128], P(('item', 'user')), may hold values from 0 to 40
- user_factors: float32 [65536, 128], P(('item', 'user')), may hold values from -6 to 6
Outputs:
- new_factors: float32 [65536, 128], P(('item', 'user'))
Inputs may be any that keep to these rules, and one draw needn't show every extreme that they name: `tile_lists`: item shard s holds tiles s * 16 to (s + 1) * 16 - 1. Among the 16 slots of one device's blocks, at most 2 name tiles of one item shard, and for some shard exactly 2 do; a tile may be named more than once.
All inputs are finite; a program needn't handle non-finite values.
Results may differ from a plain program's by a relative error of at most 0.0024.
Values sent between devices are 32-bit elements; how exact they have to be, the bound alone decides.
No kernel may reach another device: no remote copies, remote signals or barrier semaphores. Data moves between devices by JAX's collectives and lax.ppermute only.
A program may use at most 64 MiB of HBM per device.

v0:
```python
import jax
import jax.numpy as jnp
from jax import lax
from jax.sharding import PartitionSpec as P

ITERS = 4
RIDGE_WEIGHT = 0.1
EPSILON = 1e-06
HIGHEST = lax.Precision.HIGHEST


def apply_system(vectors, tiles, weights, gram):
    scores = jnp.einsum("bur,bkir->bkui", vectors, tiles, precision=HIGHEST)
    spread = jnp.einsum("bkui,bkir->bur", scores * weights, tiles, precision=HIGHEST)
    return (
        spread
        + jnp.einsum("bur,rs->bus", vectors, gram, precision=HIGHEST)
        + RIDGE_WEIGHT * vectors
    )


def conjugate(start, tiles, weights, gram, steps):
    weights = weights.astype(jnp.float32)
    target = jnp.einsum("bkui,bkir->bur", 1.0 + weights, tiles, precision=HIGHEST)
    answer = start
    resid = target - apply_system(start, tiles, weights, gram)
    direction = resid
    norm_now = jnp.sum(resid * resid, axis=-1, keepdims=True)
    for step_index in range(steps):
        image = apply_system(direction, tiles, weights, gram)
        alpha = norm_now / (jnp.sum(direction * image, axis=-1, keepdims=True) + EPSILON)
        answer = answer + alpha * direction
        resid = resid - alpha * image
        norm_next = jnp.sum(resid * resid, axis=-1, keepdims=True)
        direction = resid + norm_next / (norm_now + EPSILON) * direction
        norm_now = norm_next
    return answer


def local(item_factors, tile_lists, tile_weights, user_factors):
    factor_rank = item_factors.shape[1]
    tile_side = tile_weights.shape[-1]
    blocks_here, slots_here = tile_lists.shape
    shard_rows = item_factors.shape[0]
    user_parts = lax.axis_size("user")
    share_rows = shard_rows // user_parts
    piece = lax.dynamic_slice_in_dim(
        item_factors, lax.axis_index("user") * share_rows, share_rows, 0
    )
    partial_gram = jnp.dot(piece.T, piece, precision=HIGHEST, preferred_element_type=jnp.float32)
    gram = lax.psum(partial_gram, ("item", "user"))
    tile_ids = tile_lists.reshape(-1)
    all_rows = lax.all_gather(item_factors, "item", axis=0, tiled=True)
    fetched = all_rows.reshape(-1, tile_side, factor_rank)[tile_ids]
    tiles = fetched.reshape(blocks_here, slots_here, tile_side, factor_rank)
    start = user_factors.reshape(blocks_here, tile_side, factor_rank)
    solved = conjugate(start, tiles, tile_weights, gram, ITERS)
    return solved.reshape(-1, factor_rank)


def solution(mesh):
    in_specs = (
        P("item", None),
        P(("item", "user"), None),
        P(("item", "user"), None, None, None),
        P(("item", "user"), None),
    )
    out_specs = P(("item", "user"), None)
    return jax.shard_map(local, mesh=mesh, in_specs=in_specs, out_specs=out_specs, check_vma=False)
```

profile of v0, /device:TPU:1, one launch (start us, length us, event | category | flops | bytes accessed | tf_op | source)
XLA Modules:
  0.0 362.3 jit_solution(888267724627594206)
XLA Ops:
  7.4 0.0 all-gather.2.cloned.1.call-start
  7.4 0.7 all-gather.2.cloned.1.call-update
  8.1 0.0 all-reduce.2.cloned.1.call-start
  8.1 1.8 fusion.22
  9.9 0.0 all-reduce.2.cloned.1.call-update
  9.9 0.7 fusion.24
  10.6 1.3 copy.24
  11.9 0.9 copy.33
  12.8 101.3 %all-gather.2.cloned.1.call-done = f32[32768,128]{1,0:T(8,128)} async-done(((f32[2048,128]{1,0:T(8,128)}), f32[32768,128]{1,0:T(8,128)}) %all-gather.2.cloned.1.call-update) | async-done | bytes 16777232 | tf_op jit(solution)/shard_map/all_gather | solution.py:53
  114.2 6.4 %gather_fusion = f32[16,128,128]{2,1,0:T(8,128)S(1)} fusion(f32[256,128,128]{2,1,0:T(8,128)} %bitcast.119, s32[1024]{0:T(1024)S(1)} %pad_clamp_fusion), kind=kCustom, calls=%fused_computation | custom fusion | bytes 2097216 | tf_op jit(solution)/shard_map/gather | solution.py:54
  120.6 1.8 fusion
  122.4 1.8 convolution_bitcast_fusion.10
  124.2 1.8 convolution_bitcast_fusion.11
  126.1 211.4 %all-reduce.2.cloned.1.call-done = f32[128,128]{1,0:T(8,128)} async-done(((f32[128,128]{1,0:T(8,128)}), f32[128,128]{1,0:T(8,128)}) %all-reduce.2.cloned.1.call-update) | async-done | bytes 65552 | tf_op jit(solution)/shard_map/psum | solution.py:51
  337.5 0.0 copy-start
  337.5 1.2 fusion.12
  338.7 1.0 fusion.1
  339.7 1.8 convolution_bitcast_fusion.8
  341.5 1.1 multiply_reduce_fusion.5
  342.7 1.0 fusion.2
  343.7 1.8 convolution_bitcast_fusion.7
  345.5 1.1 multiply_reduce_fusion.3
  346.8 1.2 fusion.3
  347.9 1.8 convolution_bitcast_fusion.6
  349.8 1.1 multiply_reduce_fusion.1
  351.0 1.0 fusion.4
  352.0 1.8 convolution_bitcast_fusion.5
  353.8 0.0 copy-done
  353.8 0.3 fusion.13
  354.2 0.7 copy.43
  (15 shorter events, 0.3 us)
Async XLA Ops:
  7.4 106.8 %all-gather.2.cloned.1.call-start = ((), (), s32[]{:S(2)}) async-start(), calls=%async_computation | async-start | bytes 17825792 | tf_op jit(solution)/shard_map/all_gather | solution.py:53
  8.1 329.4 %all-reduce.2.cloned.1.call-start = ((), (), s32[]{:S(2)}) async-start(), calls=%async_computation.1 | async-start | bytes 131072 | tf_op jit(solution)/shard_map/psum | solution.py:51
  337.5 16.3 %copy-start = (f32[128,128]{1,0:T(8,128)S(1)}, f32[128,128]{1,0:T(8,128)}, u32[]{:S(2)}) copy-start(f32[128,128]{1,0:T(8,128)} %all-reduce.2.cloned.1.call-done) | copy-start | bytes 196612
Sparse Core Ops, SparseCore 0:
  10.3 103.8 all-gather.1
Sparse Core Ops, SparseCore 1:
  13.6 323.9 all-reduce.1
where the time goes:
time: 363 us; the launch traced here: 362 us
  waiting for transfers between devices  313 us (86%)
  matrix products  23.5 us (6%)
  between operations  15 us (4%)
  local copies, waits for them, and re-layouts  9.38 us (3%)
    psum x1, waiting for transfers between devices, local(): gram = lax.psum(partial_gram, ('item', 'user'))  211 us
    all_gather x1, waiting for transfers between devices, local(): all_rows = lax.all_gather(item_factors, 'item', axis=0, tiled=True)  101 us
    dot_general x5, matrix products, apply_system(): jnp.einsum('bkui,bkir->bur', scores * weights, tiles, precision=HIGHEST)  9.1 us
  transfers between devices with their start and end apart: 2, of which 2 were waited for; matrix products, arithmetic and copies ran while one was open for 5% of the time, Pallas kernels for 0%

commit v1 on v0

--- a/solution.py
+++ b/solution.py
@@ -48,7 +48,7 @@
         item_factors, lax.axis_index("user") * share_rows, share_rows, 0
     )
     partial_gram = jnp.dot(piece.T, piece, precision=HIGHEST, preferred_element_type=jnp.float32)
-    gram = lax.psum(partial_gram, ("item", "user"))
+    gram = jnp.sum(lax.all_gather(partial_gram, ("item", "user")), axis=0)
     tile_ids = tile_lists.reshape(-1)
     all_rows = lax.all_gather(item_factors, "item", axis=0, tiled=True)
     fetched = all_rows.reshape(-1, tile_side, factor_rank)[tile_ids]

time: 363 us -> 311 us (0.86)
  waiting for transfers between devices: 313 us -> 254 us
  other arithmetic: 0.93 us -> 14.2 us
    psum x1 -> x0, waiting for transfers between devices: 211 us -> none  [local(): gram = lax.psum(partial_gram, ('item', 'user'))]
    all_gather x0 -> x1, waiting for transfers between devices: none -> 152 us  [local(): gram = jnp.sum(lax.all_gather(partial_gram, ('item', 'user')), axis=0)]
    reduce_sum x0 -> x1, other arithmetic: none -> 13.3 us  [local(): gram = jnp.sum(lax.all_gather(partial_gram, ('item', 'user')), axis=0)]
where the time goes in v1:
time: 311 us
  waiting for transfers between devices  254 us (82%)
  matrix products  19.9 us (6%)
  other arithmetic  14.2 us (5%)
  between operations  13.6 us (4%)
  local copies, waits for them, and re-layouts  9.36 us (3%)
    all_gather x1, waiting for transfers between devices, local(): gram = jnp.sum(lax.all_gather(partial_gram, ('item', 'user')), axis=0)  152 us
    all_gather x1, waiting for transfers between devices, local(): all_rows = lax.all_gather(item_factors, 'item', axis=0, tiled=True)  101 us
    reduce_sum x1, other arithmetic, local(): gram = jnp.sum(lax.all_gather(partial_gram, ('item', 'user')), axis=0)  13.3 us
    dot_general x5, matrix products, apply_system(): jnp.einsum('bkui,bkir->bur', scores * weights, tiles, precision=HIGHEST)  9.1 us
    gather x1, local copies, waits for them, and re-layouts, local(): fetched = all_rows.reshape(-1, tile_side, factor_rank)[tile_ids]  6.38 us
  transfers between devices with their start and end apart: 2, of which 2 were waited for; matrix products, arithmetic and copies ran while one was open for 5% of the time, Pallas kernels for 0%

profile of v1, /device:TPU:1, one launch (start us, length us, event | category | flops | bytes accessed | tf_op | source)
XLA Modules:
  0.0 310.7 jit_solution(3241352456686290061)
XLA Ops:
  6.5 0.0 all-gather.4.cloned.1.call-start
  6.5 0.7 all-gather.4.cloned.1.call-update
  7.3 0.0 all-gather.6.cloned.1.call-start
  7.3 1.8 fusion.22
  9.1 0.0 all-gather.6.cloned.1.call-update
  9.1 0.9 copy.33
  10.0 1.3 copy.24
  11.3 0.7 fusion.24
  12.0 101.0 %all-gather.4.cloned.1.call-done = f32[32768,128]{1,0:T(8,128)} async-done(((f32[2048,128]{1,0:T(8,128)}), f32[32768,128]{1,0:T(8,128)}) %all-gather.4.cloned.1.call-update) | async-done | bytes 16777232 | tf_op jit(solution)/shard_map/all_gather | solution.py:53
  113.0 6.4 %gather_fusion = f32[16,128,128]{2,1,0:T(8,128)S(1)} fusion(f32[256,128,128]{2,1,0:T(8,128)} %bitcast.121, s32[1024]{0:T(1024)S(1)} %pad_clamp_fusion), kind=kCustom, calls=%fused_computation | custom fusion | bytes 2097216 | tf_op jit(solution)/shard_map/gather | solution.py:54
  119.4 1.8 convolution_bitcast_fusion.11
  121.2 1.8 fusion
  123.1 1.8 convolution_bitcast_fusion.10
  124.9 151.9 %all-gather.6.cloned.1.call-done = f32[65536,128]{1,0:T(8,128)} async-done(((f32[128,128]{1,0:T(8,128)}), f32[65536,128]{1,0:T(8,128)}) %all-gather.6.cloned.1.call-update) | async-done | bytes 33554448 | tf_op jit(solution)/shard_map/all_gather | solution.py:51
  276.8 0.0 copy-start
  276.8 13.3 %reduce_sum.81 = f32[128,128]{1,0:T(8,128)S(1)} reduce(f32[512,128,128]{2,1,0:T(8,128)} %bitcast.120, f32[]{:T(128)} %constant.5.clone.1), dimensions={0}, to_apply=%region_0.0 | reduce | flops 8372224 | bytes 33619972 | tf_op jit(solution)/shard_map/reduce_sum | solution.py:51
  290.1 0.0 copy-done
  290.1 0.3 fusion.12
  290.4 1.0 fusion.1
  291.4 1.8 convolution_bitcast_fusion.8
  293.2 0.3 multiply_reduce_fusion.5
  293.6 1.0 fusion.2
  294.6 1.8 convolution_bitcast_fusion.7
  296.4 0.3 multiply_reduce_fusion.3
  296.8 1.0 fusion.3
  297.8 1.8 convolution_bitcast_fusion.6
  299.6 0.3 multiply_reduce_fusion.1
  300.0 1.0 fusion.4
  301.0 1.8 convolution_bitcast_fusion.5
  302.8 0.3 fusion.13
  303.1 0.7 copy.43
  (15 shorter events, 0.3 us)
Async XLA Ops:
  6.5 106.5 %all-gather.4.cloned.1.call-start = ((), (), s32[]{:S(2)}) async-start(), calls=%async_computation | async-start | bytes 17825792 | tf_op jit(solution)/shard_map/all_gather | solution.py:53
  7.3 269.5 %all-gather.6.cloned.1.call-start = ((), (), s32[]{:S(2)}) async-start(), calls=%async_computation.1 | async-start | bytes 33619968 | tf_op jit(solution)/shard_map/all_gather | solution.py:51
  276.8 13.3 %copy-start = (f32[128,128]{1,0:T(8,128)S(1)}, f32[128,128]{1,0:T(8,128)}, u32[]{:S(2)}) copy-start(f32[128,128]{1,0:T(8,128)} %param.7) | copy-start | bytes 196612
Sparse Core Ops, SparseCore 0:
  9.4 103.5 all-gather.3
  117.5 159.2 all-gather.5

commit v2 on v0

--- a/solution.py
+++ b/solution.py
@@ -50,7 +50,9 @@
     partial_gram = jnp.dot(piece.T, piece, precision=HIGHEST, preferred_element_type=jnp.float32)
     gram = lax.psum(partial_gram, ("item", "user"))
     tile_ids = tile_lists.reshape(-1)
-    all_rows = lax.all_gather(item_factors, "item", axis=0, tiled=True)
+    all_rows = jnp.concatenate(
+        lax.all_to_all(jnp.stack([item_factors] * lax.axis_size("item")), "item", 0, 0), axis=0
+    )
     fetched = all_rows.reshape(-1, tile_side, factor_rank)[tile_ids]
     tiles = fetched.reshape(blocks_here, slots_here, tile_side, factor_rank)
     start = user_factors.reshape(blocks_here, tile_side, factor_rank)

time: 363 us -> 482 us (1.33)
  waiting for transfers between devices: 313 us -> 417 us
  starting transfers between devices: 0.05 us -> 11.9 us
  local copies, waits for them, and re-layouts: 9.38 us -> 16 us
    all_to_all x0 -> x1, waiting for transfers between devices: none -> 363 us  [local(): lax.all_to_all(jnp.stack([item_factors] * lax.axis_size('item')), 'item',...]
    psum x1, waiting for transfers between devices: 211 us -> 54.4 us  [local(): gram = lax.psum(partial_gram, ('item', 'user'))]
    all_gather x1 -> x0, waiting for transfers between devices: 101 us -> none  [local(): all_rows = lax.all_gather(item_factors, 'item', axis=0, tiled=True)]
    all_to_all x0 -> x1, starting transfers between devices: none -> 11.9 us  [local(): lax.all_to_all(jnp.stack([item_factors] * lax.axis_size('item')), 'item',...]
    another operation x0 -> x1, local copies, waits for them, and re-layouts: none -> 8.55 us  [local(): jnp.stack([item_factors] * lax.axis_size('item'))]
  transfers between devices with their start and end apart: 2 -> 2, of which waited for: 2 -> 2; matrix products, arithmetic and copies ran while one was open for 5% -> 3% of each run, Pallas kernels for 0% -> 0%
where the time goes in v2:
time: 482 us; the launch traced here: 481 us
  waiting for transfers between devices  417 us (87%)
  matrix products  22.7 us (5%)
  local copies, waits for them, and re-layouts  16 us (3%)
  between operations  13.6 us (3%)
  starting transfers between devices  11.9 us (2%)
    all_to_all x1, waiting for transfers between devices, local(): lax.all_to_all(jnp.stack([item_factors] * lax.axis_size('item')), 'item',...  363 us
    psum x1, waiting for transfers between devices, local(): gram = lax.psum(partial_gram, ('item', 'user'))  54.4 us
    all_to_all x1, starting transfers between devices, local(): lax.all_to_all(jnp.stack([item_factors] * lax.axis_size('item')), 'item',...  11.9 us
  transfers between devices with their start and end apart: 2, of which 2 were waited for; matrix products, arithmetic and copies ran while one was open for 3% of the time, Pallas kernels for 0%

profile of v2, /device:TPU:1, one launch (start us, length us, event | category | flops | bytes accessed | tf_op | source)
XLA Modules:
  0.0 481.5 jit_solution(1533136046737794364)
XLA Ops:
  6.5 8.6 %stack.2 = f32[16,2048,128]{2,1,0:T(8,128)} broadcast(f32[2048,128]{1,0:T(8,128)} %param.4), dimensions={1,2} | broadcast | bytes 17825792 | tf_op jit(solution)/shard_map/stack | solution.py:54
  15.1 0.0 copy-start.2
  15.1 11.9 %all-to-all-start = ((f32[16,2048,128]{2,1,0:T(8,128)}), f32[16,2048,128]{2,1,0:T(8,128)}, u32[]{:S(2)}, u32[]{:S(2)}) async-start(f32[16,2048,128]{2,1,0:T(8,128)} %stack.2), calls=%async_computation | async-start | bytes 33554432 | tf_op jit(solution)/shard_map/all_to_all | solution.py:54
  26.9 0.0 all-reduce.2.cloned.1.call-start
  27.0 1.8 fusion.22
  28.8 0.0 all-reduce.2.cloned.1.call-update
  28.8 0.0 copy-done.2
  28.8 0.3 copy.24
  29.1 0.0 copy-done.1
  29.1 0.1 copy.33
  29.2 0.0 copy-done.3
  29.2 362.6 %all-to-all-done = f32[16,2048,128]{2,1,0:T(8,128)} async-done(((f32[16,2048,128]{2,1,0:T(8,128)}), f32[16,2048,128]{2,1,0:T(8,128)}, u32[]{:S(2)}, u32[]{:S(2)}) %all-to-all-start) | async-done | bytes 16777248 | tf_op jit(solution)/shard_map/all_to_all | solution.py:54
  391.8 6.4 %gather_fusion = f32[16,128,128]{2,1,0:T(8,128)S(1)} fusion(f32[256,128,128]{2,1,0:T(8,128)} %bitcast.1, s32[1024]{0:T(1024)S(1)} %pad_clamp_fusion), kind=kCustom, calls=%fused_computation | custom fusion | bytes 2097216 | tf_op jit(solution)/shard_map/gather | solution.py:56
  398.2 1.0 fusion
  399.2 1.8 convolution_bitcast_fusion.10
  401.0 1.8 convolution_bitcast_fusion.11
  402.8 54.4 %all-reduce.2.cloned.1.call-done = f32[128,128]{1,0:T(8,128)} async-done(((f32[128,128]{1,0:T(8,128)}), f32[128,128]{1,0:T(8,128)}) %all-reduce.2.cloned.1.call-update) | async-done | bytes 65552 | tf_op jit(solution)/shard_map/psum | solution.py:51
  457.2 1.2 fusion.12
  458.4 1.0 fusion.1
  459.4 1.8 convolution_bitcast_fusion.8
  461.2 1.1 multiply_reduce_fusion.5
  462.5 1.0 fusion.2
  463.4 1.8 convolution_bitcast_fusion.7
  465.3 1.1 multiply_reduce_fusion.3
  466.5 1.2 fusion.3
  467.7 1.8 convolution_bitcast_fusion.6
  469.5 1.1 multiply_reduce_fusion.1
  470.7 1.0 fusion.4
  471.7 1.8 convolution_bitcast_fusion.5
  473.5 0.0 copy-done
  473.5 0.3 fusion.13
  473.9 0.7 copy.43
  (19 shorter events, 0.3 us)
Async XLA Ops:
  15.1 13.7 %copy-start.2 = (bf16[1,16,128,128]{3,2,1,0:T(8,128)(2,1)S(1)}, bf16[1,16,128,128]{3,2,1,0:T(8,128)(2,1)}, u32[]{:S(2)}) copy-start(bf16[1,16,128,128]{3,2,1,0:T(8,128)(2,1)} %param.6) | copy-start | bytes 1572868
  15.1 14.0 %copy-start.1 = (f32[128,128]{1,0:T(8,128)S(1)}, f32[128,128]{1,0:T(8,128)}, u32[]{:S(2)}) copy-start(f32[128,128]{1,0:T(8,128)} %param.7) | copy-start | bytes 196612
  15.1 14.1 %copy-start.3 = (s32[1,16]{1,0:T(1,128)S(1)}, s32[1,16]{1,0:T(1,128)}, u32[]{:S(2)}) copy-start(s32[1,16]{1,0:T(1,128)} %param.5) | copy-start | bytes 196
  15.1 376.7 %all-to-all-start = ((f32[16,2048,128]{2,1,0:T(8,128)}), f32[16,2048,128]{2,1,0:T(8,128)}, u32[]{:S(2)}, u32[]{:S(2)}) async-start(f32[16,2048,128]{2,1,0:T(8,128)} %stack.2), calls=%async_computation | async-start | bytes 33554432 | tf_op jit(solution)/shard_map/all_to_all | solution.py:54
  26.9 430.3 %all-reduce.2.cloned.1.call-start = ((), (), s32[]{:S(2)}) async-start(), calls=%async_computation.1 | async-start | bytes 131072 | tf_op jit(solution)/shard_map/psum | solution.py:51
  457.2 16.3 %copy-start = (f32[128,128]{1,0:T(8,128)S(1)}, f32[128,128]{1,0:T(8,128)}, u32[]{:S(2)}) copy-start(f32[128,128]{1,0:T(8,128)} %all-reduce.2.cloned.1.call-done) | copy-start | bytes 196612
Sparse Core Ops, SparseCore 0:
  32.7 424.4 all-reduce.1

commit v3 on v0

--- a/solution.py
+++ b/solution.py
@@ -48,7 +48,7 @@
         item_factors, lax.axis_index("user") * share_rows, share_rows, 0
     )
     partial_gram = jnp.dot(piece.T, piece, precision=HIGHEST, preferred_element_type=jnp.float32)
-    gram = lax.psum(partial_gram, ("item", "user"))
+    gram = lax.psum(lax.psum(partial_gram, "user"), "item")
     tile_ids = tile_lists.reshape(-1)
     all_rows = lax.all_gather(item_factors, "item", axis=0, tiled=True)
     fetched = all_rows.reshape(-1, tile_side, factor_rank)[tile_ids]

time: 363 us -> 299 us (0.82)
  waiting for transfers between devices: 313 us -> 250 us
    all_gather x1, waiting for transfers between devices: 101 us -> 0.03 us  [local(): all_rows = lax.all_gather(item_factors, 'item', axis=0, tiled=True)]
    psum x1 -> x2, waiting for transfers between devices: 211 us -> 249 us  [local(): gram = lax.psum(lax.psum(partial_gram, 'user'), 'item')]
  transfers between devices with their start and end apart: 2 -> 3, of which waited for: 2 -> 2; matrix products, arithmetic and copies ran while one was open for 5% -> 5% of each run, Pallas kernels for 0% -> 0%
where the time goes in v3:
time: 299 us
  waiting for transfers between devices  250 us (84%)
  matrix products  23.5 us (8%)
  between operations  15 us (5%)
  local copies, waits for them, and re-layouts  9.36 us (3%)
    psum x2, waiting for transfers between devices, local(): gram = lax.psum(lax.psum(partial_gram, 'user'), 'item')  249 us
    dot_general x5, matrix products, apply_system(): jnp.einsum('bkui,bkir->bur', scores * weights, tiles, precision=HIGHEST)  9.1 us
    gather x1, local copies, waits for them, and re-layouts, local(): fetched = all_rows.reshape(-1, tile_side, factor_rank)[tile_ids]  6.38 us
  transfers between devices with their start and end apart: 3, of which 2 were waited for; matrix products, arithmetic and copies ran while one was open for 5% of the time, Pallas kernels for 0%

profile of v3, /device:TPU:1, one launch (start us, length us, event | category | flops | bytes accessed | tf_op | source)
XLA Modules:
  0.0 298.6 jit_solution(94278415450173716)
XLA Ops:
  7.4 0.0 all-reduce.3.cloned.1.call-start
  7.4 1.8 fusion.22
  9.1 0.0 all-reduce.3.cloned.1.call-update
  9.1 0.0 all-gather.2.cloned.1.call-start
  9.2 0.5 all-gather.2.cloned.1.call-update
  9.7 0.0 all-reduce.5.cloned.1.call-start
  9.8 1.3 copy.24
  11.1 0.9 copy.33
  12.0 0.7 fusion.24
  12.7 153.0 %all-reduce.3.cloned.1.call-done = f32[128,128]{1,0:T(8,128)} async-done(((f32[128,128]{1,0:T(8,128)}), f32[128,128]{1,0:T(8,128)}) %all-reduce.3.cloned.1.call-update) | async-done | bytes 65552 | tf_op jit(solution)/shard_map/psum | solution.py:51
  165.7 0.0 all-reduce.5.cloned.1.call-update
  165.8 0.0 all-gather.2.cloned.1.call-done
  165.8 6.4 %gather_fusion = f32[16,128,128]{2,1,0:T(8,128)S(1)} fusion(f32[256,128,128]{2,1,0:T(8,128)} %bitcast.119, s32[1024]{0:T(1024)S(1)} %pad_clamp_fusion), kind=kCustom, calls=%fused_computation | custom fusion | bytes 2097216 | tf_op jit(solution)/shard_map/gather | solution.py:54
  172.2 1.8 fusion
  174.0 1.8 convolution_bitcast_fusion.10
  175.8 1.8 convolution_bitcast_fusion.11
  177.7 96.1 %all-reduce.5.cloned.1.call-done = f32[128,128]{1,0:T(8,128)} async-done(((f32[128,128]{1,0:T(8,128)}), f32[128,128]{1,0:T(8,128)}) %all-reduce.5.cloned.1.call-update) | async-done | bytes 65552 | tf_op jit(solution)/shard_map/psum | solution.py:51
  273.8 1.2 fusion.12
  275.0 1.0 fusion.1
  276.0 1.8 convolution_bitcast_fusion.8
  277.8 1.1 multiply_reduce_fusion.5
  279.0 1.0 fusion.2
  280.0 1.8 convolution_bitcast_fusion.7
  281.8 1.1 multiply_reduce_fusion.3
  283.1 1.2 fusion.3
  284.2 1.8 convolution_bitcast_fusion.6
  286.1 1.1 multiply_reduce_fusion.1
  287.3 1.0 fusion.4
  288.3 1.8 convolution_bitcast_fusion.5
  290.1 0.0 copy-done
  290.1 0.3 fusion.13
  290.5 0.7 copy.43
  (16 shorter events, 0.3 us)
Async XLA Ops:
  7.4 158.4 %all-reduce.3.cloned.1.call-start = ((), (), s32[]{:S(2)}) async-start(), calls=%async_computation.1 | async-start | bytes 131072 | tf_op jit(solution)/shard_map/psum | solution.py:51
  9.1 156.6 %all-gather.2.cloned.1.call-start = ((), (), s32[]{:S(2)}) async-start(), calls=%async_computation | async-start | bytes 17825792 | tf_op jit(solution)/shard_map/all_gather | solution.py:53
  9.7 264.1 %all-reduce.5.cloned.1.call-start = ((), (), s32[]{:S(2)}) async-start(), calls=%async_computation.2 | async-start | bytes 131072 | tf_op jit(solution)/shard_map/psum | solution.py:51
  273.8 16.3 %copy-start = (f32[128,128]{1,0:T(8,128)S(1)}, f32[128,128]{1,0:T(8,128)}, u32[]{:S(2)}) copy-start(f32[128,128]{1,0:T(8,128)} %all-reduce.5.cloned.1.call-done) | copy-start | bytes 196612
Sparse Core Ops, SparseCore 0:
  11.6 154.0 all-reduce.2
Sparse Core Ops, SparseCore 1:
  11.7 103.5 all-gather.1
  165.8 107.9 all-reduce.4
